TPU v7x, 32 devices: a whole 2x2x4 slice. The times are simulated.
32 devices in a mesh: img: 16 (over z, y, x), ref: 2 (over core).
Axes of the slice: x: 2, y: 2, z: 4, core: 2. Of those that a mesh axis runs over, the one named last changes fastest.
Arguments:
- images: bfloat16 [16384, 2048], P('img'), may hold values from -8 to 8
- references: bfloat16 [1024, 2048], P('ref'), may hold values from -1 to 1
- initial_contrast: float32 [16384], P('img'), may hold values from 0.25 to 1.75
Outputs:
- new_references: bfloat16 [1024, 2048], P('ref')
- contrast: float32 [16384], P('img')
- loglik: float32 [16384], P('img')
All inputs are finite; a program needn't handle non-finite values.
Results may differ from a plain program's by a relative error of at most 0.0041.
Values may be sent and summed in bfloat16 or wider, within the bound.
A program may use at most 64 MiB of HBM per device.

v0:
```python
import math

import jax
import jax.numpy as jnp
from jax import lax
from jax.sharding import PartitionSpec as P

ITERS = 3


sharpness = 2.0
prior_weight = 1.0
epsilon = 1e-06


def scores_of(cross_terms, ref_norms, contrast):
    contrast_col = contrast[:, None]
    return sharpness * (
        contrast_col * cross_terms - 0.5 * (contrast_col * contrast_col) * ref_norms[None, :]
    )


def statistics(cross_terms, ref_norms, contrast):
    scored = scores_of(cross_terms, ref_norms, contrast)
    highest = lax.pmax(jnp.max(scored, axis=1), "ref")
    exponent = jnp.exp(scored - highest[:, None])
    summed, weighted_cross, weighted_norm = lax.psum(
        (
            jnp.sum(exponent, axis=1),
            jnp.sum(exponent * cross_terms, axis=1),
            jnp.sum(exponent * ref_norms[None, :], axis=1),
        ),
        "ref",
    )
    return (highest, summed, weighted_cross, weighted_norm, exponent)


def normalize(sums):
    meansq = jnp.mean(sums * sums, axis=1)
    return (sums * lax.rsqrt(meansq + epsilon)[:, None]).astype(jnp.bfloat16)


def per_device(images, references, initial_contrast):
    ref_norms = jnp.sum(jnp.square(references.astype(jnp.float32)), axis=1)
    cross_terms = lax.dot_general(
        images, references, (((1,), (1,)), ((), ())), preferred_element_type=jnp.float32
    )
    contrast = initial_contrast
    for iteration in range(ITERS + 1):
        highest, summed, weighted_cross, weighted_norm, exponent = statistics(
            cross_terms, ref_norms, contrast
        )
        if iteration < ITERS:
            contrast = (weighted_cross / summed + prior_weight * initial_contrast) / (
                weighted_norm / summed + prior_weight
            )
    posterior = exponent / summed[:, None]
    weights = (posterior * contrast[:, None]).astype(jnp.bfloat16)
    own_rows = lax.psum_scatter(
        lax.dot_general(
            weights, images, (((0,), (0,)), ((), ())), preferred_element_type=jnp.float32
        ),
        "img",
        scatter_dimension=0,
        tiled=True,
    )
    gathered = lax.all_gather(normalize(own_rows), "img", axis=0, tiled=True)
    width = images.shape[1]
    new_norms = jnp.sum(jnp.square(gathered.astype(jnp.float32)), axis=1) / width
    new_cross = lax.dot_general(
        images, gathered, (((1,), (1,)), ((), ())), preferred_element_type=jnp.float32
    ) * width ** (-0.5)
    final_high, final_sum, final_cross, final_norm, final_exp = statistics(
        new_cross, new_norms, contrast
    )
    loglik = final_high + jnp.log(final_sum) - math.log(gathered.shape[0] * lax.axis_size("ref"))
    return (gathered, contrast, loglik)


def solution(mesh):
    placed = (P("img", None), P("ref", None), P("img"))
    return jax.shard_map(
        per_device,
        mesh=mesh,
        in_specs=placed,
        out_specs=(P("ref", None), P("img"), P("img")),
        check_vma=False,
    )
```

profile of v0, /device:TPU:1, one launch (start us, length us, event | category | flops | bytes accessed | tf_op | source)
XLA Modules:
  0.0 233.2 jit_solution(6979023556648752763)
XLA Ops:
  7.2 0.0 copy-start.2
  7.2 0.0 reduce-scatter.2.cloned.1.call-start
  7.2 0.0 copy-start.1
  7.2 2.2 multiply_reduce_fusion.1
  9.5 0.0 copy-done.2
  9.5 0.0 copy-done.1
  9.5 4.7 %fusion.2 = (f32[1024]{0:T(1024)S(1)}, f32[1024,512]{0,1:T(8,128)S(1)}) fusion(f32[512]{0:T(512)S(1)} %multiply_reduce_fusion.1, f32[1024]{0:T(1024)S(1)} %multiply_multiply_fusion.3, f32[1024]{0:T(1024)S(1)} %copy-done.2, bf16[1024,2048]{1,0:T(8,128)(2,1)} %param.3, bf16[512,2048]{1,0:T(8,128)(2,1)S(1)} %copy-done.1), kind=kOutput, calls=%fused_computation.21 | convolution fusion | flops 2150104064 | bytes 8402944 | tf_op jit(solution)/shard_map/dot_general | solution.py:45
  14.2 2.5 %pmax.35 = f32[1024]{0:T(1024)S(1)} all-reduce(f32[1024]{0:T(1024)S(1)} %get-tuple-element.27), channel_id=1, replica_groups=mesh['img'=16,'ref'=2] {'ref'}, use_global_device_ids=true, to_apply=%region_2.0 | all-reduce | flops 1024 | bytes 8192 | tf_op jit(solution)/shard_map/pmax | solution.py:25
  16.7 1.0 multiply_reduce_fusion.7
  17.6 3.3 %all-reduce.2 = (f32[1024]{0:T(1024)S(1)}, f32[1024]{0:T(1024)S(1)}, f32[1024]{0:T(1024)S(1)}) all-reduce(f32[1024]{0:T(1024)S(1)} %get-tuple-element.10, f32[1024]{0:T(1024)S(1)} %get-tuple-element.11, f32[1024]{0:T(1024)S(1)} %get-tuple-element.9), channel_id=1, replica_groups=mesh['img'=16,'ref'=2] {'ref'}, use_global_device_ids=true, to_apply=%region_8.0 | all-reduce | flops 3072 | bytes 24576 | tf_op jit(solution)/shard_map/psum | solution.py:27
  21.0 0.4 fusion.4
  21.4 2.5 %pmax.36 = f32[1024]{0:T(1024)S(1)} all-reduce(f32[1024]{0:T(1024)S(1)} %fusion.4), channel_id=1, replica_groups=mesh['img'=16,'ref'=2] {'ref'}, use_global_device_ids=true, to_apply=%region_10.0 | all-reduce | flops 1024 | bytes 8192 | tf_op jit(solution)/shard_map/pmax | solution.py:25
  23.9 1.0 multiply_reduce_fusion.5
  24.8 3.5 %all-reduce.1 = (f32[1024]{0:T(1024)S(1)}, f32[1024]{0:T(1024)S(1)}, f32[1024]{0:T(1024)S(1)}) all-reduce(f32[1024]{0:T(1024)S(1)} %get-tuple-element.7, f32[1024]{0:T(1024)S(1)} %get-tuple-element.8, f32[1024]{0:T(1024)S(1)} %get-tuple-element.6), channel_id=1, replica_groups=mesh['img'=16,'ref'=2] {'ref'}, use_global_device_ids=true, to_apply=%region_16.0 | all-reduce | flops 3072 | bytes 24576 | tf_op jit(solution)/shard_map/psum | solution.py:27
  28.3 0.4 fusion.6
  28.7 2.5 %pmax.37 = f32[1024]{0:T(1024)S(1)} all-reduce(f32[1024]{0:T(1024)S(1)} %fusion.6), channel_id=1, replica_groups=mesh['img'=16,'ref'=2] {'ref'}, use_global_device_ids=true, to_apply=%region_18.0 | all-reduce | flops 1024 | bytes 8192 | tf_op jit(solution)/shard_map/pmax | solution.py:25
  31.2 1.0 multiply_reduce_fusion.3
  32.2 3.3 %all-reduce = (f32[1024]{0:T(1024)S(1)}, f32[1024]{0:T(1024)S(1)}, f32[1024]{0:T(1024)S(1)}) all-reduce(f32[1024]{0:T(1024)S(1)} %get-tuple-element.4, f32[1024]{0:T(1024)S(1)} %get-tuple-element.5, f32[1024]{0:T(1024)S(1)} %get-tuple-element.3), channel_id=1, replica_groups=mesh['img'=16,'ref'=2] {'ref'}, use_global_device_ids=true, to_apply=%region_24.0 | all-reduce | flops 3072 | bytes 24576 | tf_op jit(solution)/shard_map/psum | solution.py:27
  35.5 0.0 copy-start.3
  35.5 0.4 fusion.8
  35.9 2.5 %pmax.38 = f32[1024]{0:T(1024)S(1)} all-reduce(f32[1024]{0:T(1024)S(1)} %fusion.8), channel_id=1, replica_groups=mesh['img'=16,'ref'=2] {'ref'}, use_global_device_ids=true, to_apply=%region_26.0 | all-reduce | flops 1024 | bytes 8192 | tf_op jit(solution)/shard_map/pmax | solution.py:25
  38.4 0.6 fusion.1
  39.0 2.5 %psum.86 = f32[1024]{0:T(1024)S(1)} all-reduce(f32[1024]{0:T(1024)S(1)} %fusion.1), channel_id=1, replica_groups=mesh['img'=16,'ref'=2] {'ref'}, use_global_device_ids=true, to_apply=%region_28.0 | all-reduce | flops 1024 | bytes 8192 | tf_op jit(solution)/shard_map/psum | solution.py:27
  41.5 0.0 copy-done.3
  41.5 6.8 %fusion.9 = f32[512,2048]{1,0:T(8,128)} fusion(bf16[1024,2048]{1,0:T(8,128)(2,1)} %param.3, f32[1024,512]{0,1:T(8,128)S(1)} %get-tuple-element.28, f32[1024]{0:T(1024)S(1)} %psum.86, f32[1024]{0:T(1024)S(1)} %pmax.38, f32[1024]{0:T(1024)S(1)} %multiply_multiply_fusion, f32[1024]{0:T(1024)S(1)} %get-tuple-element.35, f32[512]{0:T(512)S(1)} %multiply_reduce_fusion.1), kind=kOutput, calls=%fused_computation.28 | convolution fusion | flops 2151677952 | bytes 10504192 | tf_op jit(solution)/shard_map/dot_general | solution.py:60
  48.3 0.0 reduce-scatter.2.cloned.1.call-update
  48.3 0.2 all-gather.2.cloned.1.call-start
  48.6 96.4 %reduce-scatter.2.cloned.1.call-done = f32[32,2048]{1,0:T(8,128)} async-done(((f32[512,2048]{1,0:T(8,128)}), f32[32,2048]{1,0:T(8,128)}) %reduce-scatter.2.cloned.1.call-update) | async-done | bytes 262160 | tf_op jit(solution)/shard_map/reduce_scatter | solution.py:59
  144.9 1.1 multiply_reduce_fusion.8
  146.0 1.7 multiply_convert_fusion.2
  147.7 0.0 all-gather.2.cloned.1.call-update
  147.7 60.4 %all-gather.2.cloned.1.call-done = bf16[512,2048]{1,0:T(8,128)(2,1)} async-done(((bf16[32,2048]{1,0:T(8,128)(2,1)}), bf16[512,2048]{1,0:T(8,128)(2,1)}) %all-gather.2.cloned.1.call-update) | async-done | bytes 2097168 | tf_op jit(solution)/shard_map/all_gather | solution.py:67
  208.1 0.0 copy-start
  208.1 2.2 multiply_reduce_fusion
  210.4 0.0 copy-done
  210.4 6.0 %fusion.17 = (f32[1024]{0:T(1024)S(1)}, f32[1024,512]{0,1:T(8,128)}) fusion(f32[512]{0:T(512)S(1)} %broadcast_multiply_fusion.1, f32[1024]{0:T(1024)S(1)} %multiply_multiply_fusion, f32[1024]{0:T(1024)S(1)} %get-tuple-element.21, bf16[512,2048]{1,0:T(8,128)(2,1)S(1)} %copy-done, bf16[1024,2048]{1,0:T(8,128)(2,1)} %param.3), kind=kOutput, calls=%fused_computation.49 | convolution fusion | flops 2150104064 | bytes 8402944 | tf_op jit(solution)/shard_map/dot_general | solution.py:70
  216.4 3.7 %pmax.39 = f32[1024]{0:T(1024)S(1)} all-reduce(f32[1024]{0:T(1024)S(1)} %get-tuple-element.29), channel_id=1, replica_groups=mesh['img'=16,'ref'=2] {'ref'}, use_global_device_ids=true, to_apply=%region_33.0 | all-reduce | flops 1024 | bytes 8192 | tf_op jit(solution)/shard_map/pmax | solution.py:25
  220.1 1.9 exponential_reduce_fusion
  222.0 2.5 %psum.87 = f32[1024]{0:T(1024)S(1)} all-reduce(f32[1024]{0:T(1024)S(1)} %exponential_reduce_fusion), channel_id=1, replica_groups=mesh['img'=16,'ref'=2] {'ref'}, use_global_device_ids=true, to_apply=%region_35.0 | all-reduce | flops 1024 | bytes 8192 | tf_op jit(solution)/shard_map/psum | solution.py:27
  224.5 0.6 add_add_fusion
  225.1 1.3 copy.7
  (7 shorter events, 0.1 us)
Async XLA Ops:
  7.2 2.3 copy-start.2
  7.2 137.7 %reduce-scatter.2.cloned.1.call-start = ((), (), s32[]{:S(2)}) async-start(), calls=%async_computation.1 | async-start | bytes 4456448 | tf_op jit(solution)/shard_map/reduce_scatter | solution.py:59
  7.2 2.3 copy-start.1
  35.5 6.0 %copy-start.3 = (f32[1024]{0:T(1024)}, f32[1024]{0:T(1024)S(1)}, u32[]{:S(2)}) copy-start(f32[1024]{0:T(1024)S(1)} %get-tuple-element.35) | copy-start | bytes 12292
  48.3 159.8 %all-gather.2.cloned.1.call-start = ((), (), s32[]{:S(2)}) async-start(), calls=%async_computation.2 | async-start | bytes 2228224 | tf_op jit(solution)/shard_map/all_gather | solution.py:67
  208.1 2.2 copy-start
Sparse Core Ops, SparseCore 0:
  48.5 96.4 reduce-scatter.1
  148.3 59.8 all-gather.1
where the time goes:
time: 234 us; the launch traced here: 233 us
  waiting for transfers between devices  157 us (67%)
  blocking collectives  28.6 us (12%)
  matrix products  17.4 us (7%)
  other arithmetic  14.6 us (6%)
  between operations  14.2 us (6%)
    reduce_scatter x1, waiting for transfers between devices, per_device(): lax.psum_scatter(lax.dot_general(weights, images, (((0,), (0,)), ((), ())...  96.4 us
    all_gather x1, waiting for transfers between devices, per_device(): gathered = lax.all_gather(normalize(own_rows), 'img', axis=0, tiled=True)  60.4 us
    psum x5, blocking collectives, statistics(): lax.psum((jnp.sum(exponent, axis=1), jnp.sum(exponent * cross_terms, axis...  15 us
    pmax x5, blocking collectives, statistics(): highest = lax.pmax(jnp.max(scored, axis=1), 'ref')  13.6 us
    dot_general x1, matrix products, per_device(): lax.dot_general(weights, images, (((0,), (0,)), ((), ())), preferred_elem...  6.77 us
    dot_general x1, matrix products, per_device(): lax.dot_general(images, gathered, (((1,), (1,)), ((), ())), preferred_ele...  5.98 us
    dot_general x1, matrix products, per_device(): lax.dot_general(images, references, (((1,), (1,)), ((), ())), preferred_e...  4.69 us
  transfers between devices with their start and end apart: 2, of which 2 were waited for; matrix products, arithmetic and copies ran while one was open for 0% of the time, Pallas kernels for 0%

commit v1 on v0

v1 whole, which is shorter than its diff:
```python
import functools
import math

import jax
import jax.numpy as jnp
from jax import lax
from jax.experimental import pallas as pl
from jax.experimental.pallas import tpu as pltpu
from jax.sharding import PartitionSpec as P

ITERS = 3

sharpness = 2.0
prior_weight = 1.0
epsilon = 1e-06

MESH = pl.DeviceIdType.MESH
LANES = 256
QUADS = ((1, 0), (1, 1), (0, 1), (0, 0))
F32 = jnp.float32
BF16 = jnp.bfloat16


def kernel(
    nz, n_ref, im_hbm, ref_hbm, prior_ref, newref_hbm, contrast_ref, loglik_ref,
    im, refs, norms, cross, w, snd1, rcv1, acc, snd2, rcv2, snd3, rcv3, gath,
    stat_snd, stat_rcv, vecs, im_sem, ref_sem, out_sem, ssem, rsem,
):
    n, width = im.shape
    rows = refs.shape[0]
    rb = rows // (4 * nz)
    qr = nz * rb
    half = width // 2
    me = lax.axis_index("img")
    rme = lax.axis_index("ref")
    x, y, z = lax.rem(me, 2), lax.rem(me // 2, 2), me // 4
    counter = [0]

    def chip(dx, dy, dz):
        return lax.rem(z + dz, nz) * 4 + lax.rem(y + dy, 2) * 2 + lax.rem(x + dx, 2)

    def send(src, dst, dev):
        i = counter[0]
        counter[0] += 1
        copy = pltpu.make_async_remote_copy(
            src_ref=src, dst_ref=dst, send_sem=ssem.at[i], recv_sem=rsem.at[i],
            device_id=dev, device_id_type=MESH,
        )
        copy.start()
        sent.append(copy)
        return copy

    sent = []
    x_dev = {"img": chip(1, 0, 0)}
    y_dev = {"img": chip(0, 1, 0)}
    z_dev = [{"img": chip(0, 0, k)} for k in range(nz)]
    r_dev = [{"ref": lax.rem(rme + k, n_ref)} for k in range(n_ref)]

    ref_copies = []
    for q, (dx, dy) in enumerate(QUADS):
        for dz in range(nz):
            s = q * nz + dz
            copy = pltpu.make_async_copy(
                ref_hbm.at[pl.ds(chip(dx, dy, dz) * rb, rb)],
                refs.at[pl.ds(s * rb, rb)], ref_sem.at[s],
            )
            copy.start()
            ref_copies.append(copy)
    im_copies = []
    for b in range(n // LANES):
        part = pl.ds(b * LANES, LANES)
        copy = pltpu.make_async_copy(im_hbm.at[part], im.at[part], im_sem.at[b])
        copy.start()
        im_copies.append(copy)

    barrier = pltpu.get_barrier_semaphore()
    peers = [x_dev, y_dev] + z_dev[1:] + r_dev[1:]
    for dev in peers:
        pl.semaphore_signal(barrier, inc=1, device_id=dev, device_id_type=MESH)

    stat_snd[...] = jnp.zeros_like(stat_snd)
    vecs[0:1, :] = prior_ref[...]

    def square_sums(source, r0, count, scale):
        block = source[r0 : r0 + count, :].astype(F32)
        total = jnp.sum(block * block, axis=1, keepdims=True) * scale
        norms[r0 : r0 + count, :] = jnp.broadcast_to(total, (count, LANES))

    for s, copy in enumerate(ref_copies):
        copy.wait()
        square_sums(refs, s * rb, rb, 1.0)

    nt = (((1,), (1,)), ((), ()))
    nn = (((1,), (0,)), ((), ()))
    for copy in im_copies:
        copy.wait()

    def score_block(source, r0, count, scale):
        def body(b, carry):
            part = pl.ds(pl.multiple_of(b * LANES, LANES), LANES)
            out = lax.dot_general(
                source[r0 : r0 + count, :], im[part, :], nt, preferred_element_type=F32
            )
            cross[r0 : r0 + count, part] = out if scale is None else out * scale
            return carry

        lax.fori_loop(0, n // LANES, body, 0)

    score_block(refs, 0, rows, None)
    pl.semaphore_wait(barrier, len(peers))

    def scored(part):
        a = vecs[0:1, part]
        c = cross[:, part]
        return c, sharpness * (a * c - (0.5 * (a * a)) * norms[...])

    def statistics(it, full):
        def body(b, carry):
            part = pl.ds(pl.multiple_of(b * LANES, LANES), LANES)
            c, s = scored(part)
            top = jnp.max(s, axis=0, keepdims=True)
            e = jnp.exp(s - top)
            stat_snd[it, 0:1, part] = top
            stat_snd[it, 1:2, part] = jnp.sum(e, axis=0, keepdims=True)
            if full:
                stat_snd[it, 2:3, part] = jnp.sum(e * c, axis=0, keepdims=True)
                stat_snd[it, 3:4, part] = jnp.sum(e * norms[...], axis=0, keepdims=True)
            return carry

        lax.fori_loop(0, n // LANES, body, 0)
        copies = [
            send(stat_snd.at[it], stat_rcv.at[it * (n_ref - 1) + k - 1], r_dev[k])
            for k in range(1, n_ref)
        ]
        for copy in copies:
            copy.wait_recv()
        blocks = [stat_snd[it]] + [
            stat_rcv[it * (n_ref - 1) + k - 1] for k in range(1, n_ref)
        ]
        high = functools.reduce(jnp.maximum, [blk[0:1] for blk in blocks])
        scales = [jnp.exp(blk[0:1] - high) for blk in blocks]
        sums = [
            functools.reduce(jnp.add, [blk[j : j + 1] * sc for blk, sc in zip(blocks, scales)])
            for j in ((1, 2, 3) if full else (1,))
        ]
        return high, sums

    for it in range(ITERS):
        high, (total, along, weight) = statistics(it, True)
        vecs[0:1, :] = (along / total + prior_weight * prior_ref[...]) / (
            weight / total + prior_weight
        )
    high, (total,) = statistics(ITERS, False)
    vecs[1:2, :] = high
    vecs[2:3, :] = vecs[0:1, :] / total
    contrast_ref[...] = vecs[0:1, :]

    def weigh(b, carry):
        part = pl.ds(pl.multiple_of(b * LANES, LANES), LANES)
        _, s = scored(part)
        w[:, part] = (jnp.exp(s - vecs[1:2, part]) * vecs[2:3, part]).astype(BF16)
        return carry

    lax.fori_loop(0, n // LANES, weigh, 0)

    def weighted(r0s, c0, store):
        def body(b, carry):
            col = pl.multiple_of(b * LANES, LANES)
            lhs = [w[r0 : r0 + cnt, :] for r0, cnt in r0s]
            lhs = lhs[0] if len(lhs) == 1 else jnp.concatenate(lhs, axis=0)
            rhs = im[:, pl.ds(pl.multiple_of(c0 + col, LANES), LANES)]
            out = lax.dot_general(lhs, rhs, nn, preferred_element_type=F32)
            store(pl.ds(col, LANES), out[:qr], out[qr:])
            return carry

        lax.fori_loop(0, half // LANES, body, 0)

    def to_send(stream, first_is_far):
        def store(cols, lo, hi):
            far, near = (lo, hi) if first_is_far else (hi, lo)
            snd1[stream * 2, :, cols] = far.astype(BF16)
            snd1[stream * 2 + 1, :, cols] = near.astype(BF16)

        return store

    def to_keep(stream):
        def store(cols, lo, hi):
            acc[stream * 2, :, cols] = lo
            acc[stream * 2 + 1, :, cols] = hi

        return store

    weighted([(0, 2 * qr)], 0, to_send(0, False))
    step1 = [[send(snd1.at[j], rcv1.at[j], x_dev) for j in (0, 1)]]
    weighted([(qr, 2 * qr)], half, to_send(1, True))
    step1.append([send(snd1.at[j], rcv1.at[j], y_dev) for j in (2, 3)])
    weighted([(2 * qr, 2 * qr)], 0, to_keep(0))
    weighted([(0, qr), (3 * qr, qr)], half, to_keep(1))

    z_order = sorted(range(1, nz), key=lambda k: (min(k, nz - k), k))
    far_order = z_order[::-1]
    step2 = [{}, {}]
    for s, dev in ((0, y_dev), (1, x_dev)):
        step1[s][0].wait_recv()
        snd2[s] = (acc[s * 2] + rcv1[s * 2].astype(F32)).astype(BF16)
        for dz in far_order + [0]:
            part = pl.ds(dz * rb, rb)
            step2[s][dz] = send(snd2.at[s, part], rcv2.at[s, part], dev)
    for s in (0, 1):
        step1[s][1].wait_recv()
        acc[s * 2 + 1] = acc[s * 2 + 1] + rcv1[s * 2 + 1].astype(F32)
    step3 = []
    for dz in far_order:
        r0 = dz * rb
        for s in (0, 1):
            step2[s][dz].wait_recv()
            snd3[s, dz - 1] = (
                acc[s * 2 + 1, r0 : r0 + rb, :] + rcv2[s, r0 : r0 + rb, :].astype(F32)
            ).astype(BF16)
            step3.append((s, dz, send(snd3.at[s, dz - 1], rcv3.at[s, dz - 1], z_dev[dz])))
    for s in (0, 1):
        step2[s][0].wait_recv()
        acc[s * 2 + 1, 0:rb, :] = acc[s * 2 + 1, 0:rb, :] + rcv2[s, 0:rb, :].astype(F32)
    for s, dz, copy in step3:
        copy.wait_recv()
        acc[s * 2 + 1, 0:rb, :] = acc[s * 2 + 1, 0:rb, :] + rcv3[s, dz - 1].astype(F32)

    left, right = acc[1, 0:rb, :], acc[3, 0:rb, :]
    square = jnp.sum(left * left, axis=1, keepdims=True) + jnp.sum(
        right * right, axis=1, keepdims=True
    )
    factor = lax.rsqrt(square / width + epsilon)
    own = 3 * qr
    gath[own : own + rb, 0:half] = (left * factor).astype(BF16)
    gath[own : own + rb, half:width] = (right * factor).astype(BF16)

    def piece(q, dz, s):
        return gath.at[pl.ds(q * qr + dz * rb, rb), pl.ds(s * half, half)]

    def slot(q, dz):
        return gath.at[pl.ds(q * qr + dz * rb, rb)]

    along_z = {}
    for k in far_order:
        along_z[nz - k] = send(slot(3, 0), slot(3, nz - k), z_dev[k])
    into_x, into_y, last = {}, {}, []

    def spread(dz):
        into_y[dz] = [send(piece(3, dz, 0), piece(2, dz, 0), y_dev)]
        into_x[dz] = [send(piece(3, dz, 1), piece(0, dz, 1), x_dev)]
        into_y[dz].append(send(piece(3, dz, 1), piece(2, dz, 1), y_dev))
        into_x[dz].append(send(piece(3, dz, 0), piece(0, dz, 0), x_dev))

    def forward(dz):
        into_y[dz][0].wait_recv()
        last.append(send(piece(2, dz, 0), piece(1, dz, 0), x_dev))
        into_x[dz][0].wait_recv()
        last.append(send(piece(0, dz, 1), piece(1, dz, 1), y_dev))

    outs = []

    def rescore(q):
        dx, dy = QUADS[q]
        for dz in range(nz):
            copy = pltpu.make_async_copy(
                slot(q, dz), newref_hbm.at[pl.ds(chip(dx, dy, dz) * rb, rb)],
                out_sem.at[q * nz + dz],
            )
            copy.start()
            outs.append(copy)
        score_block(gath, q * qr, qr, width ** (-0.5))
        square_sums(gath, q * qr, qr, 1.0 / width)

    spread(0)
    before = 0
    for dz in z_order:
        along_z[dz].wait_recv()
        spread(dz)
        if dz == z_order[-1]:
            forward(before)
            rescore(3)
            forward(dz)
        else:
            forward(before)
        before = dz
    if not z_order:
        rescore(3)
        forward(0)
    for q, into in ((0, into_x), (2, into_y)):
        for dz in range(nz):
            j = 1 if q == 0 else 1
            into[dz][j].wait_recv()
        rescore(q)
    for copy in last:
        copy.wait_recv()
    rescore(1)

    high, (total,) = statistics(ITERS + 1, False)
    loglik_ref[...] = high + jnp.log(total) - math.log(rows * n_ref)
    for copy in outs:
        copy.wait()
    for copy in sent:
        copy.wait_send()


def per_device(nz, n_ref, images, references, initial_contrast):
    n, width = images.shape
    rows = references.shape[0]
    rb = rows // (4 * nz)
    qr, half = nz * rb, width // 2
    steps = ITERS + 2
    copies = steps * (n_ref - 1) + 4 + 2 * nz + 2 * (nz - 1) + (nz - 1) + 6 * nz
    peers = max(n_ref - 1, 1)
    flops = 6 * n * width * rows
    new_references, contrast, loglik = pl.pallas_call(
        functools.partial(kernel, nz, n_ref),
        out_shape=(
            jax.ShapeDtypeStruct((rows, width), BF16),
            jax.ShapeDtypeStruct((1, n), F32),
            jax.ShapeDtypeStruct((1, n), F32),
        ),
        in_specs=[
            pl.BlockSpec(memory_space=pl.ANY),
            pl.BlockSpec(memory_space=pl.ANY),
            pl.BlockSpec(memory_space=pltpu.VMEM),
        ],
        out_specs=(
            pl.BlockSpec(memory_space=pl.ANY),
            pl.BlockSpec(memory_space=pltpu.VMEM),
            pl.BlockSpec(memory_space=pltpu.VMEM),
        ),
        scratch_shapes=[
            pltpu.VMEM((n, width), BF16),
            pltpu.VMEM((rows, width), BF16),
            pltpu.VMEM((rows, LANES), F32),
            pltpu.VMEM((rows, n), F32),
            pltpu.VMEM((rows, n), BF16),
            pltpu.VMEM((4, qr, half), BF16),
            pltpu.VMEM((4, qr, half), BF16),
            pltpu.VMEM((4, qr, half), F32),
            pltpu.VMEM((2, qr, half), BF16),
            pltpu.VMEM((2, qr, half), BF16),
            pltpu.VMEM((2, max(nz - 1, 1), rb, half), BF16),
            pltpu.VMEM((2, max(nz - 1, 1), rb, half), BF16),
            pltpu.VMEM((rows, width), BF16),
            pltpu.VMEM((steps, 8, n), F32),
            pltpu.VMEM((steps * peers, 8, n), F32),
            pltpu.VMEM((8, n), F32),
            pltpu.SemaphoreType.DMA((n // LANES,)),
            pltpu.SemaphoreType.DMA((4 * nz,)),
            pltpu.SemaphoreType.DMA((4 * nz,)),
            pltpu.SemaphoreType.DMA((copies,)),
            pltpu.SemaphoreType.DMA((copies,)),
        ],
        compiler_params=pltpu.CompilerParams(
            collective_id=0, has_side_effects=True, vmem_limit_bytes=56 * 1024 * 1024
        ),
        cost_estimate=pl.CostEstimate(
            flops=flops, bytes_accessed=2 * n * width, transcendentals=0
        ),
    )(images, references, initial_contrast[None, :])
    return (new_references, contrast[0], loglik[0])


def solution(mesh):
    n_img, n_ref = mesh.shape["img"], mesh.shape["ref"]
    placed = (P("img", None), P("ref", None), P("img"))
    return jax.shard_map(
        functools.partial(per_device, n_img // 4, n_ref),
        mesh=mesh,
        in_specs=placed,
        out_specs=(P("ref", None), P("img"), P("img")),
        check_vma=False,
    )
```

time: 234 us -> 88.9 us (0.38)
  the two profiles are of different devices: /device:TPU:1 before, /device:TPU:9 now
where the time goes in v1:
time: 88.9 us; the launch traced here: 88.7 us
  Pallas kernels  83.7 us (94%)
  local copies, waits for them, and re-layouts  4.36 us (5%)
    pallas_call x1, Pallas kernels, per_device(): pl.pallas_call(functools.partial(kernel, nz, n_ref), out_shape=(jax.Shape...  83.7 us
    unnamed x7, local copies, waits for them, and re-layouts  4.36 us

profile of v1, /device:TPU:9, one launch (start us, length us, event | category | flops | bytes accessed | tf_op | source)
XLA Modules:
  0.0 88.7 jit_solution(9598682527922045415)
XLA Ops:
  0.6 83.7 %shard_map.58 = (bf16[512,2048]{1,0:T(8,128)(2,1)}, f32[1,1024]{1,0:T(1,128)}, f32[1,1024]{1,0:T(1,128)}) custom-call(bf16[1024,2048]{1,0:T(8,128)(2,1)} %im_hbm.1, bf16[512,2048]{1,0:T(8,128)(2,1)} %ref_hbm.1, f32[1,1024]{1,0:T(1,128)} %bitcast.5), custom_call_target="tpu_custom_call" | custom-call | flops 6442450944 | bytes 4194304 | tf_op jit(solution)/shard_map/pallas_call | solution.py:315
  84.3 0.0 copy-start.1
  84.4 0.0 copy-start
  84.4 3.2 %copy.9 = bf16[512,2048]{1,0:T(8,128)(2,1)} copy(bf16[512,2048]{1,0:T(8,128)(2,1)} %get-tuple-element.12) | data formatting | bytes 4194304
  87.5 0.0 copy-done.1
  87.5 0.6 copy.10
  88.1 0.0 copy-done
  88.1 0.6 copy.11
Async XLA Ops:
  84.3 3.2 %copy-start.1 = (f32[1,1024]{1,0:T(1,128)S(1)}, f32[1,1024]{1,0:T(1,128)}, u32[]{:S(2)}) copy-start(f32[1,1024]{1,0:T(1,128)} %get-tuple-element.7) | copy-start | bytes 12292
  84.4 3.8 %copy-start = (f32[1,1024]{1,0:T(1,128)S(1)}, f32[1,1024]{1,0:T(1,128)}, u32[]{:S(2)}) copy-start(f32[1,1024]{1,0:T(1,128)} %get-tuple-element.8) | copy-start | bytes 12292

commit v2 on v1

--- a/solution.py
+++ b/solution.py
@@ -37,7 +37,12 @@
     counter = [0]
 
     def chip(dx, dy, dz):
-        return lax.rem(z + dz, nz) * 4 + lax.rem(y + dy, 2) * 2 + lax.rem(x + dx, 2)
+        zz, bit = z, 1
+        while bit < nz:
+            if dz & bit:
+                zz = zz + bit - 2 * bit * lax.rem(z // bit, 2)
+            bit *= 2
+        return zz * 4 + lax.rem(y + dy, 2) * 2 + lax.rem(x + dx, 2)
 
     def send(src, dst, dev):
         i = counter[0]
@@ -74,7 +79,7 @@
         im_copies.append(copy)
 
     barrier = pltpu.get_barrier_semaphore()
-    peers = [x_dev, y_dev] + z_dev[1:] + r_dev[1:]
+    peers = [x_dev, y_dev] + [z_dev[k] for k in range(1, nz) if k & (k - 1) == 0] + r_dev[1:]
     for dev in peers:
         pl.semaphore_signal(barrier, inc=1, device_id=dev, device_id_type=MESH)
 
@@ -190,40 +195,74 @@
 
         return store
 
+    low = [dz & -dz for dz in range(nz)]
+    order = sorted(range(1, nz), key=lambda k: (low[k], -k)) + [0]
+    early = [dz for dz in order if low[dz] == 1] or order
+    late = [dz for dz in order if dz not in early]
+    hop_dev = (x_dev, y_dev)
+    step1 = {}
+
+    def send1(s, j, dzs):
+        for dz in dzs:
+            part = pl.ds(dz * rb, rb)
+            step1[s, j, dz] = send(
+                snd1.at[s * 2 + j, part], rcv1.at[s * 2 + j, part], hop_dev[s]
+            )
+
     weighted([(0, 2 * qr)], 0, to_send(0, False))
-    step1 = [[send(snd1.at[j], rcv1.at[j], x_dev) for j in (0, 1)]]
+    send1(0, 0, early)
+    send1(0, 1, early)
     weighted([(qr, 2 * qr)], half, to_send(1, True))
-    step1.append([send(snd1.at[j], rcv1.at[j], y_dev) for j in (2, 3)])
+    send1(1, 0, early)
+    send1(1, 1, early)
     weighted([(2 * qr, 2 * qr)], 0, to_keep(0))
     weighted([(0, qr), (3 * qr, qr)], half, to_keep(1))
 
-    z_order = sorted(range(1, nz), key=lambda k: (min(k, nz - k), k))
-    far_order = z_order[::-1]
-    step2 = [{}, {}]
-    for s, dev in ((0, y_dev), (1, x_dev)):
-        step1[s][0].wait_recv()
-        snd2[s] = (acc[s * 2] + rcv1[s * 2].astype(F32)).astype(BF16)
-        for dz in far_order + [0]:
-            part = pl.ds(dz * rb, rb)
-            step2[s][dz] = send(snd2.at[s, part], rcv2.at[s, part], dev)
+    step2 = {}
+
+    def send2(dzs):
+        for dz in dzs:
+            r0 = dz * rb
+            part = pl.ds(r0, rb)
+            for s in (1, 0):
+                step1[s, 0, dz].wait_recv()
+                snd2[s, r0 : r0 + rb, :] = (
+                    acc[s * 2, r0 : r0 + rb, :] + rcv1[s * 2, r0 : r0 + rb, :].astype(F32)
+                ).astype(BF16)
+                step2[s, dz] = send(snd2.at[s, part], rcv2.at[s, part], hop_dev[1 - s])
+
+    def gained(s, dz):
+        step1[s, 1, dz].wait_recv()
+        step2[s, dz].wait_recv()
+        r0 = dz * rb
+        return (
+            acc[s * 2 + 1, r0 : r0 + rb, :]
+            + rcv1[s * 2 + 1, r0 : r0 + rb, :].astype(F32)
+            + rcv2[s, r0 : r0 + rb, :].astype(F32)
+        )
+
+    send2(early)
+    for j in (0, 1):
+        for s in (0, 1):
+            send1(s, j, late)
+    send2(late)
+
+    step3 = {}
+
+    def complete(s, dz):
+        total = gained(s, dz)
+        for k in range(nz):
+            if low[k] and k - low[k] == dz and (dz == 0 or low[k] < low[dz]):
+                step3[s, k].wait_recv()
+                total = total + rcv3[s, k - 1].astype(F32)
+        return total
+
+    for dz in order[:-1]:
+        for s in (0, 1):
+            snd3[s, dz - 1] = complete(s, dz).astype(BF16)
+            step3[s, dz] = send(snd3.at[s, dz - 1], rcv3.at[s, dz - 1], z_dev[low[dz]])
     for s in (0, 1):
-        step1[s][1].wait_recv()
-        acc[s * 2 + 1] = acc[s * 2 + 1] + rcv1[s * 2 + 1].astype(F32)
-    step3 = []
-    for dz in far_order:
-        r0 = dz * rb
-        for s in (0, 1):
-            step2[s][dz].wait_recv()
-            snd3[s, dz - 1] = (
-                acc[s * 2 + 1, r0 : r0 + rb, :] + rcv2[s, r0 : r0 + rb, :].astype(F32)
-            ).astype(BF16)
-            step3.append((s, dz, send(snd3.at[s, dz - 1], rcv3.at[s, dz - 1], z_dev[dz])))
-    for s in (0, 1):
-        step2[s][0].wait_recv()
-        acc[s * 2 + 1, 0:rb, :] = acc[s * 2 + 1, 0:rb, :] + rcv2[s, 0:rb, :].astype(F32)
-    for s, dz, copy in step3:
-        copy.wait_recv()
-        acc[s * 2 + 1, 0:rb, :] = acc[s * 2 + 1, 0:rb, :] + rcv3[s, dz - 1].astype(F32)
+        acc[s * 2 + 1, 0:rb, :] = complete(s, 0)
 
     left, right = acc[1, 0:rb, :], acc[3, 0:rb, :]
     square = jnp.sum(left * left, axis=1, keepdims=True) + jnp.sum(
@@ -241,8 +280,12 @@
         return gath.at[pl.ds(q * qr + dz * rb, rb)]
 
     along_z = {}
-    for k in far_order:
-        along_z[nz - k] = send(slot(3, 0), slot(3, nz - k), z_dev[k])
+
+    def double(dz, bits):
+        for bit in bits:
+            along_z[dz + bit] = send(slot(3, dz), slot(3, dz + bit), z_dev[bit])
+
+    bits = [1 << j for j in range(nz.bit_length() - 1)]
     into_x, into_y, last = {}, {}, []
 
     def spread(dz):
@@ -259,41 +302,38 @@
 
     outs = []
 
-    def rescore(q):
-        dx, dy = QUADS[q]
-        for dz in range(nz):
-            copy = pltpu.make_async_copy(
-                slot(q, dz), newref_hbm.at[pl.ds(chip(dx, dy, dz) * rb, rb)],
-                out_sem.at[q * nz + dz],
-            )
-            copy.start()
-            outs.append(copy)
-        score_block(gath, q * qr, qr, width ** (-0.5))
-        square_sums(gath, q * qr, qr, 1.0 / width)
-
+    def rescore(q0, count):
+        for q in range(q0, q0 + count):
+            dx, dy = QUADS[q]
+            for dz in range(nz):
+                copy = pltpu.make_async_copy(
+                    slot(q, dz), newref_hbm.at[pl.ds(chip(dx, dy, dz) * rb, rb)],
+                    out_sem.at[q * nz + dz],
+                )
+                copy.start()
+                outs.append(copy)
+        score_block(gath, q0 * qr, count * qr, width ** (-0.5))
+        square_sums(gath, q0 * qr, count * qr, 1.0 / width)
+
+    double(0, bits)
     spread(0)
+    arrivals = sorted(range(1, nz), key=lambda k: (k.bit_count(), k))
     before = 0
-    for dz in z_order:
+    for dz in arrivals:
         along_z[dz].wait_recv()
+        double(dz, [bit for bit in bits if bit < low[dz]])
         spread(dz)
-        if dz == z_order[-1]:
-            forward(before)
-            rescore(3)
-            forward(dz)
-        else:
-            forward(before)
+        forward(before)
         before = dz
-    if not z_order:
-        rescore(3)
-        forward(0)
-    for q, into in ((0, into_x), (2, into_y)):
-        for dz in range(nz):
-            j = 1 if q == 0 else 1
-            into[dz][j].wait_recv()
-        rescore(q)
+    forward(before)
+    for dz in range(nz):
+        into_y[dz][1].wait_recv()
+    rescore(2, 2)
+    for dz in range(nz):
+        into_x[dz][1].wait_recv()
     for copy in last:
         copy.wait_recv()
-    rescore(1)
+    rescore(0, 2)
 
     high, (total,) = statistics(ITERS + 1, False)
     loglik_ref[...] = high + jnp.log(total) - math.log(rows * n_ref)
@@ -309,7 +349,7 @@
     rb = rows // (4 * nz)
     qr, half = nz * rb, width // 2
     steps = ITERS + 2
-    copies = steps * (n_ref - 1) + 4 + 2 * nz + 2 * (nz - 1) + (nz - 1) + 6 * nz
+    copies = steps * (n_ref - 1) + 6 * nz + 2 * (nz - 1) + (nz - 1) + 6 * nz
     peers = max(n_ref - 1, 1)
     flops = 6 * n * width * rows
     new_references, contrast, loglik = pl.pallas_call(

time: 88.9 us -> 78.9 us (0.89)
  the two profiles are of different devices: /device:TPU:9 before, /device:TPU:1 now
where the time goes in v2:
time: 78.9 us; the launch traced here: 78.7 us
  Pallas kernels  73.7 us (93%)
  local copies, waits for them, and re-layouts  4.36 us (6%)
    pallas_call x1, Pallas kernels, per_device(): pl.pallas_call(functools.partial(kernel, nz, n_ref), out_shape=(jax.Shape...  73.7 us
    unnamed x7, local copies, waits for them, and re-layouts  4.36 us

profile of v2, /device:TPU:1, one launch (start us, length us, event | category | flops | bytes accessed | tf_op | source)
XLA Modules:
  0.0 78.7 jit_solution(12005502337525026917)
XLA Ops:
  0.6 73.7 %shard_map.58 = (bf16[512,2048]{1,0:T(8,128)(2,1)}, f32[1,1024]{1,0:T(1,128)}, f32[1,1024]{1,0:T(1,128)}) custom-call(bf16[1024,2048]{1,0:T(8,128)(2,1)} %im_hbm.1, bf16[512,2048]{1,0:T(8,128)(2,1)} %ref_hbm.1, f32[1,1024]{1,0:T(1,128)} %bitcast.5), custom_call_target="tpu_custom_call" | custom-call | flops 6442450944 | bytes 4194304 | tf_op jit(solution)/shard_map/pallas_call | solution.py:355
  74.4 0.0 copy-start.1
  74.4 0.0 copy-start
  74.4 3.2 %copy.9 = bf16[512,2048]{1,0:T(8,128)(2,1)} copy(bf16[512,2048]{1,0:T(8,128)(2,1)} %get-tuple-element.12) | data formatting | bytes 4194304
  77.5 0.0 copy-done.1
  77.5 0.6 copy.10
  78.1 0.0 copy-done
  78.1 0.6 copy.11
Async XLA Ops:
  74.4 3.2 %copy-start.1 = (f32[1,1024]{1,0:T(1,128)S(1)}, f32[1,1024]{1,0:T(1,128)}, u32[]{:S(2)}) copy-start(f32[1,1024]{1,0:T(1,128)} %get-tuple-element.7) | copy-start | bytes 12292
  74.4 3.8 %copy-start = (f32[1,1024]{1,0:T(1,128)S(1)}, f32[1,1024]{1,0:T(1,128)}, u32[]{:S(2)}) copy-start(f32[1,1024]{1,0:T(1,128)} %get-tuple-element.8) | copy-start | bytes 12292

commit v3 on v2

--- a/solution.py
+++ b/solution.py
@@ -117,7 +117,7 @@
     def scored(part):
         a = vecs[0:1, part]
         c = cross[:, part]
-        return c, sharpness * (a * c - (0.5 * (a * a)) * norms[...])
+        return c, (sharpness * a) * c - ((0.5 * sharpness) * (a * a)) * norms[...]
 
     def statistics(it, full):
         def body(b, carry):
@@ -241,12 +241,6 @@
             + rcv2[s, r0 : r0 + rb, :].astype(F32)
         )
 
-    send2(early)
-    for j in (0, 1):
-        for s in (0, 1):
-            send1(s, j, late)
-    send2(late)
-
     step3 = {}
 
     def complete(s, dz):
@@ -257,10 +251,22 @@
                 total = total + rcv3[s, k - 1].astype(F32)
         return total
 
-    for dz in order[:-1]:
+    def send3(dzs):
+        for dz in dzs:
+            for s in (0, 1):
+                snd3[s, dz - 1] = complete(s, dz).astype(BF16)
+                step3[s, dz] = send(
+                    snd3.at[s, dz - 1], rcv3.at[s, dz - 1], z_dev[low[dz]]
+                )
+
+    send2(early)
+    for j in (0, 1):
         for s in (0, 1):
-            snd3[s, dz - 1] = complete(s, dz).astype(BF16)
-            step3[s, dz] = send(snd3.at[s, dz - 1], rcv3.at[s, dz - 1], z_dev[low[dz]])
+            send1(s, j, late)
+    if late:
+        send3(early)
+    send2(late)
+    send3([dz for dz in late if dz])
     for s in (0, 1):
         acc[s * 2 + 1, 0:rb, :] = complete(s, 0)
 
@@ -355,9 +361,9 @@
     new_references, contrast, loglik = pl.pallas_call(
         functools.partial(kernel, nz, n_ref),
         out_shape=(
-            jax.ShapeDtypeStruct((rows, width), BF16),
-            jax.ShapeDtypeStruct((1, n), F32),
-            jax.ShapeDtypeStruct((1, n), F32),
+            pltpu.VMEM((rows, width), BF16),
+            pltpu.VMEM((1, n), F32),
+            pltpu.VMEM((1, n), F32),
         ),
         in_specs=[
             pl.BlockSpec(memory_space=pl.ANY),
@@ -365,7 +371,7 @@
             pl.BlockSpec(memory_space=pltpu.VMEM),
         ],
         out_specs=(
-            pl.BlockSpec(memory_space=pl.ANY),
+            pl.BlockSpec(memory_space=pltpu.VMEM),
             pl.BlockSpec(memory_space=pltpu.VMEM),
             pl.BlockSpec(memory_space=pltpu.VMEM),
         ),
@@ -383,8 +389,8 @@
             pltpu.VMEM((2, max(nz - 1, 1), rb, half), BF16),
             pltpu.VMEM((2, max(nz - 1, 1), rb, half), BF16),
             pltpu.VMEM((rows, width), BF16),
-            pltpu.VMEM((steps, 8, n), F32),
-            pltpu.VMEM((steps * peers, 8, n), F32),
+            pltpu.VMEM((steps, 4, n), F32),
+            pltpu.VMEM((steps * peers, 4, n), F32),
             pltpu.VMEM((8, n), F32),
             pltpu.SemaphoreType.DMA((n // LANES,)),
             pltpu.SemaphoreType.DMA((4 * nz,)),

time: 78.9 us -> 77.5 us (0.982)
  local copies, waits for them, and re-layouts: 4.36 us -> 2.51 us
    unnamed x7 -> x3, local copies, waits for them, and re-layouts: 4.36 us -> 2.51 us
where the time goes in v3:
time: 77.5 us; the launch traced here: 77.3 us
  Pallas kernels  74.1 us (96%)
  local copies, waits for them, and re-layouts  2.51 us (3%)
    pallas_call x1, Pallas kernels, per_device(): pl.pallas_call(functools.partial(kernel, nz, n_ref), out_shape=(pltpu.VME...  74.1 us
    unnamed x3, local copies, waits for them, and re-layouts  2.51 us

profile of v3, /device:TPU:1, one launch (start us, length us, event | category | flops | bytes accessed | tf_op | source)
XLA Modules:
  0.0 77.3 jit_solution(10216621970197995656)
XLA Ops:
  0.6 74.1 %shard_map.58 = (bf16[512,2048]{1,0:T(8,128)(2,1)S(1)}, f32[1,1024]{1,0:T(1,128)S(1)}, f32[1,1024]{1,0:T(1,128)S(1)}) custom-call(bf16[1024,2048]{1,0:T(8,128)(2,1)} %im_hbm.1, bf16[512,2048]{1,0:T(8,128)(2,1)} %ref_hbm.1, f32[1,1024]{1,0:T(1,128)} %bitcast.5), custom_call_target="tpu_custom_call" | custom-call | flops 6442450944 | bytes 4194304 | tf_op jit(solution)/shard_map/pallas_call | solution.py:361
  74.8 1.3 %copy.9 = bf16[512,2048]{1,0:T(8,128)(2,1)} copy(bf16[512,2048]{1,0:T(8,128)(2,1)S(1)} %get-tuple-element.9) | data formatting | bytes 4194304
  76.1 0.6 copy.10
  76.7 0.6 copy.11

commit v4 on v3

--- a/solution.py
+++ b/solution.py
@@ -260,13 +260,18 @@
                 )
 
     send2(early)
-    for j in (0, 1):
+    middle = [dz for dz in late if dz]
+    final = [dz for dz in late if not dz]
+    for j, dzs in ((0, middle), (1, middle), (0, final)):
         for s in (0, 1):
-            send1(s, j, late)
+            send1(s, j, dzs)
     if late:
         send3(early)
-    send2(late)
-    send3([dz for dz in late if dz])
+    send2(middle)
+    for s in (0, 1):
+        send1(s, 1, final)
+    send2(final)
+    send3(middle)
     for s in (0, 1):
         acc[s * 2 + 1, 0:rb, :] = complete(s, 0)
 
@@ -308,18 +313,16 @@
 
     outs = []
 
-    def rescore(q0, count):
-        for q in range(q0, q0 + count):
-            dx, dy = QUADS[q]
-            for dz in range(nz):
-                copy = pltpu.make_async_copy(
-                    slot(q, dz), newref_hbm.at[pl.ds(chip(dx, dy, dz) * rb, rb)],
-                    out_sem.at[q * nz + dz],
-                )
-                copy.start()
-                outs.append(copy)
-        score_block(gath, q0 * qr, count * qr, width ** (-0.5))
-        square_sums(gath, q0 * qr, count * qr, 1.0 / width)
+    def finish(q):
+        dx, dy = QUADS[q]
+        for dz in range(nz):
+            copy = pltpu.make_async_copy(
+                slot(q, dz), newref_hbm.at[pl.ds(chip(dx, dy, dz) * rb, rb)],
+                out_sem.at[q * nz + dz],
+            )
+            copy.start()
+            outs.append(copy)
+        square_sums(gath, q * qr, qr, 1.0 / width)
 
     double(0, bits)
     spread(0)
@@ -334,12 +337,16 @@
     forward(before)
     for dz in range(nz):
         into_y[dz][1].wait_recv()
-    rescore(2, 2)
+    finish(3)
+    finish(2)
+    score_block(gath, 2 * qr, 2 * qr, width ** (-0.5))
     for dz in range(nz):
         into_x[dz][1].wait_recv()
+    finish(0)
     for copy in last:
         copy.wait_recv()
-    rescore(0, 2)
+    finish(1)
+    score_block(gath, 0, 2 * qr, width ** (-0.5))
 
     high, (total,) = statistics(ITERS + 1, False)
     loglik_ref[...] = high + jnp.log(total) - math.log(rows * n_ref)

time: 77.5 us -> 75.7 us (0.977)
  Pallas kernels: 74.1 us -> 72.4 us
    pallas_call x1, Pallas kernels: 74.1 us -> 72.4 us  [per_device(): pl.pallas_call(functools.partial(kernel, nz, n_ref), out_shape=(pltpu.VME...]
where the time goes in v4:
time: 75.7 us; the launch traced here: 75.5 us
  Pallas kernels  72.4 us (96%)
  local copies, waits for them, and re-layouts  2.51 us (3%)
    pallas_call x1, Pallas kernels, per_device(): pl.pallas_call(functools.partial(kernel, nz, n_ref), out_shape=(pltpu.VME...  72.4 us
    unnamed x3, local copies, waits for them, and re-layouts  2.51 us

profile of v4, /device:TPU:1, one launch (start us, length us, event | category | flops | bytes accessed | tf_op | source)
XLA Modules:
  0.0 75.5 jit_solution(11038105640280352735)
XLA Ops:
  0.6 72.4 %shard_map.58 = (bf16[512,2048]{1,0:T(8,128)(2,1)S(1)}, f32[1,1024]{1,0:T(1,128)S(1)}, f32[1,1024]{1,0:T(1,128)S(1)}) custom-call(bf16[1024,2048]{1,0:T(8,128)(2,1)} %im_hbm.1, bf16[512,2048]{1,0:T(8,128)(2,1)} %ref_hbm.1, f32[1,1024]{1,0:T(1,128)} %bitcast.5), custom_call_target="tpu_custom_call" | custom-call | flops 6442450944 | bytes 4194304 | tf_op jit(solution)/shard_map/pallas_call | solution.py:368
  73.0 1.3 %copy.9 = bf16[512,2048]{1,0:T(8,128)(2,1)} copy(bf16[512,2048]{1,0:T(8,128)(2,1)S(1)} %get-tuple-element.9) | data formatting | bytes 4194304
  74.3 0.6 copy.10
  74.9 0.6 copy.11
